TPU v7x, 512 devices: a whole 4x8x8 slice. The times are simulated.
512 devices in a mesh: row: 64 (over y, z_hi, core), hid: 8 (over z_lo, x).
Axes of the slice: x: 4, y: 8, z: 8 (z_hi: 4, z_lo: 2; z = z_hi * 2 + z_lo), core: 2. Of those that a mesh axis runs over, the one named last changes fastest.
Arguments:
- features: bfloat16 [256, 256, 512], P('row'), may hold values from -6 to 6
- dw_weight: float32 [2, 7, 7, 512], replicated, may hold values from -0.875 to 0.875
- dw_bias: float32 [2, 512], replicated, may hold values from -3 to 3
- ln_gain: float32 [2, 512], replicated, may hold values from 0.1 to 1.9
- ln_bias: float32 [2, 512], replicated, may hold values from -3 to 3
- w_up: bfloat16 [2, 512, 2048], P(None, None, 'hid'), may hold values from -0.25 to 0.25
- b_up: float32 [2, 2048], P(None, 'hid'), may hold values from -3 to 3
- w_down: bfloat16 [2, 2048, 512], P(None, 'hid'), may hold values from -0.125 to 0.125
- b_down: float32 [2, 512], replicated, may hold values from -3 to 3
- layer_scale: float32 [2, 512], replicated, may hold values from 0.2 to 1
Outputs:
- result_map: bfloat16 [256, 256, 512], P('row')
All inputs are finite; a program needn't handle non-finite values.
Results may differ from a plain program's by a relative error of at most 0.018.
Values may be sent and summed in bfloat16 or wider, within the bound.
A program may use at most 64 MiB of HBM per device.

v0:
```python
import jax
import jax.numpy as jnp
from jax import lax
from jax.sharding import PartitionSpec as P


def extended(block, sides, width):
    for axis, dim in sides:
        count = lax.axis_size(axis)
        forward = [(i, i + 1) for i in range(count - 1)]
        backward = [(target, source) for source, target in forward]
        low = lax.ppermute(
            lax.slice_in_dim(block, block.shape[dim] - width, None, axis=dim), axis, forward
        )
        high = lax.ppermute(lax.slice_in_dim(block, 0, width, axis=dim), axis, backward)
        block = jnp.concatenate([low, block, high], axis=dim)
    return block


def depthwise(padded, kernel, bias):
    pad = kernel.shape[0] // 2
    rows = padded.shape[0] - 2 * pad
    width = padded.shape[1]
    wide = jnp.pad(padded, ((0, 0), (pad, pad), (0, 0)))
    total = jnp.zeros((rows, width, padded.shape[2]), jnp.float32)
    for i in range(kernel.shape[0]):
        for j in range(kernel.shape[1]):
            total = total + wide[i : i + rows, j : j + width, :].astype(jnp.float32) * kernel[i, j]
    return (total + bias).astype(jnp.bfloat16)


def expand(conv, gain, shift, w_first, b_first):
    values = conv.reshape(-1, conv.shape[2]).astype(jnp.float32)
    mean = jnp.mean(values, axis=1, keepdims=True)
    var = jnp.mean((values - mean) ** 2, axis=1, keepdims=True)
    normed = ((values - mean) / jnp.sqrt(var + 1e-06) * gain + shift).astype(jnp.bfloat16)
    return jax.nn.gelu(
        jnp.dot(normed, w_first, preferred_element_type=jnp.float32) + b_first, approximate=False
    ).astype(jnp.bfloat16)


def pointwise(conv, gain, shift, w_first, b_first, w_second):
    hidden = expand(conv, gain, shift, w_first, b_first)
    partial_sum = jnp.dot(hidden, w_second, preferred_element_type=jnp.float32)
    return partial_sum.reshape(conv.shape[0], conv.shape[1], -1)


def shards(features, dw_weight, dw_bias, ln_gain, ln_bias, w_up, b_up, w_down, b_down, layer_scale):
    reach = dw_weight.shape[1] // 2
    state = features
    for b in range(dw_weight.shape[0]):
        padded = extended(state, (("row", 0),), reach)
        conv = depthwise(padded, dw_weight[b], dw_bias[b])
        partial_sum = pointwise(conv, ln_gain[b], ln_bias[b], w_up[b], b_up[b], w_down[b])
        summed = lax.psum(partial_sum.astype(jnp.bfloat16), "hid").astype(jnp.float32)
        state = (state.astype(jnp.float32) + layer_scale[b] * (summed + b_down[b])).astype(
            jnp.bfloat16
        )
    return state


def solution(mesh):
    return jax.shard_map(
        shards,
        mesh=mesh,
        in_specs=(
            P("row", None, None),
            P(),
            P(),
            P(),
            P(),
            P(None, None, "hid"),
            P(None, "hid"),
            P(None, "hid", None),
            P(),
            P(),
        ),
        out_specs=P("row", None, None),
        check_vma=False,
    )
```

profile of v0, /device:TPU:16, one launch (start us, length us, event | category | flops | bytes accessed | tf_op | source)
XLA Modules:
  0.0 296.9 jit_solution(8753654461528168947)
XLA Ops:
  6.6 1.6 fusion.99
  8.2 2.1 collective-permute-start
  10.2 10.3 %collective-permute-start.1 = (bf16[3,256,512]{2,1,0:T(8,128)(2,1)S(1)}, bf16[3,256,512]{2,1,0:T(8,128)(2,1)S(1)}, u32[]{:S(2)}, u32[]{:S(2)}) collective-permute-start(bf16[3,256,512]{2,1,0:T(8,128)(2,1)S(1)} %get-tuple-element.14), channel_id=1, source_target_pairs={{8,0},{16,8},{24,16},{32,24},{40,32},{48,40},{56,48},{64,56},{72,6... | collective-permute-start | bytes 2359304 | tf_op jit(solution)/shard_map/ppermute | solution.py:15
  20.9 14.3 %collective-permute-done = bf16[3,256,512]{2,1,0:T(8,128)(2,1)S(1)} collective-permute-done((bf16[3,256,512]{2,1,0:T(8,128)(2,1)S(1)}, bf16[3,256,512]{2,1,0:T(8,128)(2,1)S(1)}, u32[]{:S(2)}, u32[]{:S(2)}) %collective-permute-start) | collective-permute-done | bytes 786464 | tf_op jit(solution)/shard_map/ppermute | solution.py:12
  35.4 1.9 collective-permute-done.1
  37.3 0.8 select_maximum_fusion.2
  38.2 16.1 %convert_reduce_fusion.1 = (f32[4,256]{1,0:T(4,128)S(1)}, bf16[4,256,512]{2,1,0:T(8,128)(2,1)S(1)}) fusion(f32[512]{0:T(512)S(1)} %bitcast.241, f32[512]{0:T(512)S(1)} %bitcast.171, bf16[10,262,512]{2,1,0:T(8,128)(2,1)S(1)} %select_maximum_fusion.2, f32[512]{0:T(512)S(1)} %bitcast.172, f32[512]{0:T(512)S(1)} %bitcast.173, f32[512]{0:T(512)S(1)} %bitcast.174, ...), kind=kLoop, calls=%fused_computation.13 | loop fusion | flops 78642176 | bytes 52535296 | tf_op jit(solution)/shard_map/reduce_sum | solution.py:34
  54.4 0.5 fusion.10
  55.4 2.7 fusion.68
  58.1 1.4 convolution_convert_fusion.1
  59.7 90.1 %all-reduce.5.cloned.1.call-done = bf16[4,256,512]{2,1,0:T(8,128)(2,1)} async-done(((bf16[4,256,512]{2,1,0:T(8,128)(2,1)}), bf16[4,256,512]{2,1,0:T(8,128)(2,1)}) %all-reduce.5.cloned.1.call-update) | async-done | bytes 1048592 | tf_op jit(solution)/shard_map/psum | solution.py:55
  149.8 1.6 fusion.39
  151.5 1.9 collective-permute-start.2
  153.5 6.8 %collective-permute-start.3 = (bf16[3,256,512]{2,1,0:T(8,128)(2,1)S(1)}, bf16[3,256,512]{2,1,0:T(8,128)(2,1)S(1)}, u32[]{:S(2)}, u32[]{:S(2)}) collective-permute-start(bf16[3,256,512]{2,1,0:T(8,128)(2,1)S(1)} %get-tuple-element.10), channel_id=1, source_target_pairs={{8,0},{16,8},{24,16},{32,24},{40,32},{48,40},{56,48},{64,56},{72,6... | collective-permute-start | bytes 2359304 | tf_op jit(solution)/shard_map/ppermute | solution.py:15
  160.4 14.7 %collective-permute-done.2 = bf16[3,256,512]{2,1,0:T(8,128)(2,1)S(1)} collective-permute-done((bf16[3,256,512]{2,1,0:T(8,128)(2,1)S(1)}, bf16[3,256,512]{2,1,0:T(8,128)(2,1)S(1)}, u32[]{:S(2)}, u32[]{:S(2)}) %collective-permute-start.2) | collective-permute-done | bytes 786464 | tf_op jit(solution)/shard_map/ppermute | solution.py:12
  175.1 2.7 collective-permute-done.3
  177.8 0.8 select_maximum_fusion
  178.7 16.3 %convert_reduce_fusion = (f32[4,256]{1,0:T(4,128)S(1)}, bf16[4,256,512]{2,1,0:T(8,128)(2,1)S(1)}) fusion(f32[512]{0:T(512)S(1)} %bitcast.238, f32[512]{0:T(512)S(1)} %bitcast.201, bf16[10,262,512]{2,1,0:T(8,128)(2,1)S(1)} %select_maximum_fusion, f32[512]{0:T(512)S(1)} %bitcast.202, f32[512]{0:T(512)S(1)} %bitcast.203, f32[512]{0:T(512)S(1)} %bitcast.204, ...), kind=kLoop, calls=%fused_computation.9 | loop fusion | flops 81787904 | bytes 47816704 | tf_op jit(solution)/shard_map/reduce_sum | solution.py:34
  194.9 0.5 fusion.6
  195.5 0.5 fusion.9
  196.0 2.7 fusion.71
  198.7 1.4 convolution_convert_fusion
  200.1 87.4 %all-reduce.7.cloned.1.call-done = bf16[4,256,512]{2,1,0:T(8,128)(2,1)} async-done(((bf16[4,256,512]{2,1,0:T(8,128)(2,1)}), bf16[4,256,512]{2,1,0:T(8,128)(2,1)}) %all-reduce.7.cloned.1.call-update) | async-done | bytes 1048592 | tf_op jit(solution)/shard_map/psum | solution.py:55
  287.5 2.6 fusion.65
  (47 shorter events, 1.5 us)
Async XLA Ops:
  6.5 14.0 %copy-start.2 = (f32[2,7,7,512]{3,0,2,1:T(2,128)S(1)}, f32[2,7,7,512]{3,0,2,1:T(2,128)}, u32[]{:S(2)}) copy-start(f32[2,7,7,512]{3,0,2,1:T(2,128)} %param.11) | copy-start | bytes 602116
  6.5 14.2 %copy-start.3 = (f32[2,512]{1,0:T(2,128)S(1)}, f32[2,512]{1,0:T(2,128)}, u32[]{:S(2)}) copy-start(f32[2,512]{1,0:T(2,128)} %param.12) | copy-start | bytes 12292
  6.5 14.2 %copy-start.4 = (f32[2,512]{1,0:T(2,128)S(1)}, f32[2,512]{1,0:T(2,128)}, u32[]{:S(2)}) copy-start(f32[2,512]{1,0:T(2,128)} %param.13) | copy-start | bytes 12292
  6.5 14.3 %copy-start.5 = (f32[2,512]{1,0:T(2,128)S(1)}, f32[2,512]{1,0:T(2,128)}, u32[]{:S(2)}) copy-start(f32[2,512]{1,0:T(2,128)} %param.14) | copy-start | bytes 12292
  6.5 14.3 %copy-start.8 = (f32[2,256]{1,0:T(2,128)S(1)}, f32[2,256]{1,0:T(2,128)}, u32[]{:S(2)}) copy-start(f32[2,256]{1,0:T(2,128)} %param.16) | copy-start | bytes 6148
  6.5 143.2 %all-reduce.5.cloned.1.call-start = ((), (), s32[]{:S(2)}) async-start(), calls=%async_computation | async-start | bytes 2097152 | tf_op jit(solution)/shard_map/psum | solution.py:55
  8.2 27.1 %copy-start = (bf16[4,256,512]{2,1,0:T(8,128)(2,1)S(1)}, bf16[4,256,512]{2,1,0:T(8,128)(2,1)}, u32[]{:S(2)}) copy-start(bf16[4,256,512]{2,1,0:T(8,128)(2,1)} %param.10) | copy-start | bytes 3145732
  8.2 27.0 %collective-permute-start = (bf16[3,256,512]{2,1,0:T(8,128)(2,1)S(1)}, bf16[3,256,512]{2,1,0:T(8,128)(2,1)S(1)}, u32[]{:S(2)}, u32[]{:S(2)}) collective-permute-start(bf16[3,256,512]{2,1,0:T(8,128)(2,1)S(1)} %get-tuple-element.13), channel_id=1, source_target_pairs={{0,8},{8,16},{16,24},{24,32},{32,40},{40,48},{48,56},{56,64},{64,7... | collective-permute-start | bytes 2359304 | tf_op jit(solution)/shard_map/ppermute | solution.py:12
  10.2 27.1 %collective-permute-start.1 = (bf16[3,256,512]{2,1,0:T(8,128)(2,1)S(1)}, bf16[3,256,512]{2,1,0:T(8,128)(2,1)S(1)}, u32[]{:S(2)}, u32[]{:S(2)}) collective-permute-start(bf16[3,256,512]{2,1,0:T(8,128)(2,1)S(1)} %get-tuple-element.14), channel_id=1, source_target_pairs={{8,0},{16,8},{24,16},{32,24},{40,32},{48,40},{56,48},{64,56},{72,6... | collective-permute-start | bytes 2359304 | tf_op jit(solution)/shard_map/ppermute | solution.py:15
  54.3 1.0 copy-start.9
  55.4 2.8 copy-start.1
  58.1 1.5 copy-start.6
  58.1 1.5 copy-start.7
  59.6 227.9 %all-reduce.7.cloned.1.call-start = ((), (), s32[]{:S(2)}) async-start(), calls=%async_computation.1 | async-start | bytes 2097152 | tf_op jit(solution)/shard_map/psum | solution.py:55
  151.5 23.6 %collective-permute-start.2 = (bf16[3,256,512]{2,1,0:T(8,128)(2,1)S(1)}, bf16[3,256,512]{2,1,0:T(8,128)(2,1)S(1)}, u32[]{:S(2)}, u32[]{:S(2)}) collective-permute-start(bf16[3,256,512]{2,1,0:T(8,128)(2,1)S(1)} %get-tuple-element.9), channel_id=1, source_target_pairs={{0,8},{8,16},{16,24},{24,32},{32,40},{40,48},{48,56},{56,64},{64,7... | collective-permute-start | bytes 2359304 | tf_op jit(solution)/shard_map/ppermute | solution.py:12
  153.5 24.3 %collective-permute-start.3 = (bf16[3,256,512]{2,1,0:T(8,128)(2,1)S(1)}, bf16[3,256,512]{2,1,0:T(8,128)(2,1)S(1)}, u32[]{:S(2)}, u32[]{:S(2)}) collective-permute-start(bf16[3,256,512]{2,1,0:T(8,128)(2,1)S(1)} %get-tuple-element.10), channel_id=1, source_target_pairs={{8,0},{16,8},{24,16},{32,24},{40,32},{48,40},{56,48},{64,56},{72,6... | collective-permute-start | bytes 2359304 | tf_op jit(solution)/shard_map/ppermute | solution.py:15
Sparse Core Ops, SparseCore 0:
  59.7 90.0 all-reduce.4
  200.2 87.2 all-reduce.6
where the time goes:
time: 297 us
  waiting for transfers between devices  211 us (71%)
  other arithmetic  40.2 us (14%)
  starting transfers between devices  21.1 us (7%)
  between operations  13.8 us (5%)
  matrix products  8.25 us (3%)
    psum x2, waiting for transfers between devices, shards(): lax.psum(partial_sum.astype(jnp.bfloat16), 'hid').astype(jnp.float32)  178 us
    reduce_sum x2, other arithmetic, expand(): mean = jnp.mean(values, axis=1, keepdims=True)  32.3 us
    ppermute x2, waiting for transfers between devices, extended(): lax.ppermute(lax.slice_in_dim(block, block.shape[dim] - width, None, axis...  29 us
    ppermute x2, starting transfers between devices, extended(): lax.ppermute(lax.slice_in_dim(block, 0, width, axis=dim), axis, backward)  17.1 us
  transfers between devices with their start and end apart: 6, of which 6 were waited for; matrix products, arithmetic and copies ran while one was open for 0% of the time, Pallas kernels for 0%

commit v1 on v0

v1 whole, which is shorter than its diff:
```python
import functools

import jax
import jax.numpy as jnp
from jax import lax
from jax.experimental import pallas as pl
from jax.experimental.pallas import tpu as pltpu
from jax.sharding import PartitionSpec as P

MESH = pl.DeviceIdType.MESH
C, F, COLS, OWN, WIDE = 512, 256, 256, 32, 48
X, Y, ZH = 4, 8, 4
LANES = C // 128


def kernel(
    features, dww, dwb, gain, shift, w_up, b_up, w_down, b_down, scale, out,
    w, bup, xin, xf, conv, normed, acc, state, halo,
    load_sem, x1_send, x1_recv, x2_send, x2_recv, z_send, z_recv, y_send, y_recv, p_send, p_recv,
    b_send, b_recv, f_send, f_recv, h_send, h_recv, g_send, g_recv,
):
    row, hid = lax.axis_index("row"), lax.axis_index("hid")
    y, zh, core = row // 8, (row // 2) % 4, row % 2
    zl, x = hid // 4, hid % 4
    parity = y % 2

    def at(r, h):
        return {"row": r, "hid": h}

    def share(k):
        kk = k % 4
        return ((zl + k // 4) % 2) * 4 + (x + kk + (kk // 2) * (5 - 2 * kk)) % 4

    def place(h):
        return (h // 4) * 7 + (1 - 2 * (h // 4)) * (h % 4)

    right, left = at(row, zl * 4 + (x + 1) % 4), at(row, zl * 4 + (x + 3) % 4)
    twin = at(row, (1 - zl) * 4 + x)
    zh_up, zh_down = (zh + zl) % 4, (zh + 3 + zl) % 4
    z_up = at(y * 8 + zh_up * 2 + core, (1 - zl) * 4 + x)
    z_down = at(y * 8 + zh_down * 2 + core, (1 - zl) * 4 + x)
    y_up, y_down = at((row + 8) % 64, hid), at((row + 56) % 64, hid)
    partner = at(y * 8 + zh * 2 + 1 - core, hid)
    below, above = at((row + 1) % 64, hid), at((row + 63) % 64, hid)
    peers = [at(row, (hid + d) % 8) for d in range(1, 8)]
    far_z = at(y * 8 + ((zh + 3 + 2 * zl) % 4) * 2 + core, (1 - zl) * 4 + x)
    far_row = at((row + 63 + 2 * core) % 64, hid)

    mine = place(hid)
    start = jnp.clip(mine * OWN - 16, 0, COLS - 64)
    into = pl.multiple_of(start - mine * OWN + 32, 16)
    start = pl.multiple_of(start, 16)

    loads = []
    for b in range(2):
        for c in range(2):
            loads.append((w_up.at[b, pl.ds(256 * c, 256), :], w.at[b, hid, c, 0:256, :], load_sem.at[4 * b + 2 * c]))
            loads.append((w_down.at[b, :, pl.ds(256 * c, 256)], w.at[b, hid, c, 256:512, :], load_sem.at[4 * b + 2 * c + 1]))
    loads.append((features.at[:, pl.ds(start, 64), :], xin.at[3:7, pl.ds(into, 64), :], load_sem.at[8]))
    loads.append((b_up, bup.at[hid], load_sem.at[9]))
    loads = [pltpu.make_async_copy(*load) for load in loads]
    for load in loads:
        load.start()

    @pl.when(mine == 0)
    def _():
        xin[:, 16:32, :] = jnp.zeros((10, 16, C), jnp.bfloat16)

    @pl.when(mine == 7)
    def _():
        xin[:, 64:80, :] = jnp.zeros((10, 16, C), jnp.bfloat16)

    barrier = pltpu.get_barrier_semaphore()
    greeted = peers + [far_z, y_up, y_down, partner, far_row]
    for device in greeted:
        pl.semaphore_signal(barrier, inc=1, device_id=device, device_id_type=MESH)
    pl.semaphore_wait(barrier, len(greeted))

    sent = []

    def send(src, dst, send_sem, recv_sem, device):
        copy = pltpu.make_async_remote_copy(
            src_ref=src, dst_ref=dst, send_sem=send_sem, recv_sem=recv_sem, device_id=device, device_id_type=MESH
        )
        copy.start()
        sent.append(copy)

    def arrived(dst, send_sem, recv_sem):
        pltpu.make_async_remote_copy(
            src_ref=dst, dst_ref=dst, send_sem=send_sem, recv_sem=recv_sem, device_id=partner, device_id_type=MESH
        ).wait_recv()

    def part(b, k, at_core, first=0, count=512):
        return w.at[b, share(k), at_core, pl.ds(first, count), :]

    def pass_on(ref, send_sem, recv_sem, device):
        send(ref, ref, send_sem, recv_sem, device)

    def x1(b):
        pass_on(part(b, 0, core, 0, 256), x1_send.at[b, 0], x1_recv.at[b, 0], right)
        pass_on(part(b, 0, core, 256, 256), x1_send.at[b, 2], x1_recv.at[b, 2], left)
        pass_on(part(b, 0, core, 256, 256), x1_send.at[b, 1], x1_recv.at[b, 1], right)
        pass_on(part(b, 0, core, 0, 256), x1_send.at[b, 3], x1_recv.at[b, 3], left)

    def x2(b):
        arrived(part(b, 2, core, 0, 256), x1_send.at[b, 0], x1_recv.at[b, 0])
        pass_on(part(b, 2, core, 0, 256), x2_send.at[b, 0], x2_recv.at[b, 0], right)
        arrived(part(b, 1, core, 256, 256), x1_send.at[b, 2], x1_recv.at[b, 2])
        pass_on(part(b, 1, core, 256, 256), x2_send.at[b, 1], x2_recv.at[b, 1], left)

    def x1_rest(b):
        arrived(part(b, 2, core, 256, 256), x1_send.at[b, 1], x1_recv.at[b, 1])
        arrived(part(b, 1, core, 0, 256), x1_send.at[b, 3], x1_recv.at[b, 3])

    def x2_rest(b):
        arrived(part(b, 3, core, 0, 256), x2_send.at[b, 0], x2_recv.at[b, 0])
        arrived(part(b, 3, core, 256, 256), x2_send.at[b, 1], x2_recv.at[b, 1])

    def quarter(b, k, near, from_up):
        first = 256 * (parity if near else 1 - parity) + 128 * from_up
        return part(b, k, core, pl.multiple_of(first, 128), 128)

    def z(b, k):
        pass_on(quarter(b, k, True, 0), z_send.at[b, k, 0], z_recv.at[b, k, 0], z_up)
        pass_on(quarter(b, k, True, 1), z_send.at[b, k, 1], z_recv.at[b, k, 1], z_down)

    def yy(b, k):
        arrived(quarter(b, k + 4, True, 0), z_send.at[b, k, 0], z_recv.at[b, k, 0])
        pass_on(quarter(b, k + 4, True, 0), y_send.at[b, k, 0], y_recv.at[b, k, 0], y_up)
        arrived(quarter(b, k + 4, True, 1), z_send.at[b, k, 1], z_recv.at[b, k, 1])
        pass_on(quarter(b, k + 4, True, 1), y_send.at[b, k, 1], y_recv.at[b, k, 1], y_down)

    def y_rest(b, k):
        for side in range(2):
            arrived(quarter(b, k + 4, False, side), y_send.at[b, k, side], y_recv.at[b, k, side])

    def to_partner(b, k):
        pass_on(part(b, k, core), p_send.at[b, k - 1], p_recv.at[b, k - 1], partner)

    def from_partner(b, k):
        arrived(part(b, k, 1 - core), p_send.at[b, k - 1], p_recv.at[b, k - 1])

    for load in loads:
        load.wait()
    x1(0)
    z(0, 0)
    window = xin.at[3:7, pl.ds(into, 64), :]
    send(xin.at[4:7, pl.ds(into, 64), :], xin.at[0:3, pl.ds(into, 64), :], f_send.at[0], f_recv.at[0], below)
    send(xin.at[3:6, pl.ds(into, 64), :], xin.at[7:10, pl.ds(into, 64), :], f_send.at[1], f_recv.at[1], above)
    for n, peer in enumerate(peers):
        send(bup.at[hid], bup.at[hid], b_send.at[n], b_recv.at[n], peer)

    def convolve(b, columns, offset):
        def one(g, _):
            lanes = pl.ds(pl.multiple_of(g * 128, 128), 128)
            total = [jnp.zeros((columns, 128), jnp.float32) + dwb[b : b + 1, lanes] for _ in range(4)]
            for j in range(7):
                for i in range(10):
                    value = xf[g, i, pl.ds(offset - 3 + j, columns), :]
                    for r in range(max(0, i - 6), min(3, i) + 1):
                        total[r] = total[r] + value * dww[b, i - r, j : j + 1, lanes]
            for r in range(4):
                conv[pl.ds(r * columns, columns), lanes] = total[r]
            return 0

        lax.fori_loop(0, LANES, one, 0)

        def norm(t, _):
            rows = pl.ds(pl.multiple_of(t * 32, 32), 32)
            values = conv[rows, :].astype(jnp.bfloat16).astype(jnp.float32)
            mean = jnp.mean(values, axis=1, keepdims=True)
            var = jnp.mean((values - mean) ** 2, axis=1, keepdims=True)
            result = (values - mean) / jnp.sqrt(var + 1e-06) * gain[b : b + 1, :] + shift[b : b + 1, :]
            normed[rows, :] = result.astype(jnp.bfloat16)
            return 0

        lax.fori_loop(0, columns * 4 // 32, norm, 0)
        acc[0 : columns * 4, :] = jnp.zeros((columns * 4, C), jnp.float32) + b_down[b : b + 1, :]

    def pointwise(b, count, first, last):
        def one(k, _):
            s = share(k)
            up = jnp.dot(normed[0:count, 0:256], w[b, s, 0, 0:256, :], preferred_element_type=jnp.float32)
            up = up + jnp.dot(normed[0:count, 256:512], w[b, s, 1, 0:256, :], preferred_element_type=jnp.float32)
            up = up + bup[s, b : b + 1, :]
            hidden = (0.5 * up * (1.0 + lax.erf(up * 0.5**0.5))).astype(jnp.bfloat16)
            for c in range(2):
                lanes = slice(256 * c, 256 * c + 256)
                acc[0:count, lanes] += jnp.dot(hidden, w[b, s, c, 256:512, :], preferred_element_type=jnp.float32)
            return 0

        lax.fori_loop(first, last, one, 0)

    for side in range(2):
        arrived(xin.at[pl.ds(7 * side, 3), pl.ds(into, 64), :], f_send.at[side], f_recv.at[side])

    @pl.when(row == 0)
    def _():
        xin[0:3, :, :] = jnp.zeros((3, 96, C), jnp.bfloat16)

    @pl.when(row == 63)
    def _():
        xin[7:10, :, :] = jnp.zeros((3, 96, C), jnp.bfloat16)

    def widen(i, _):
        for g in range(LANES):
            xf[g, i, :, :] = xin[i, 16:80, 128 * g : 128 * g + 128].astype(jnp.float32)
        return 0

    lax.fori_loop(0, 10, widen, 0)
    convolve(0, WIDE, 8)
    x2(0)
    x1(1)
    z(1, 0)
    yy(0, 0)
    for n, peer in enumerate(peers):
        origin = (hid + 7 - n) % 8
        arrived(bup.at[origin], b_send.at[n], b_recv.at[n])
    pointwise(0, 4 * WIDE, 0, 1)
    x1_rest(0)
    for k in (1, 2):
        z(0, k)
        to_partner(0, k)
    y_rest(0, 0)
    to_partner(0, 4)
    x2_rest(0)
    z(0, 3)
    to_partner(0, 3)
    yy(0, 1)
    yy(0, 2)
    yy(1, 0)
    for k in (1, 2):
        from_partner(0, k)
    pointwise(0, 4 * WIDE, 1, 3)
    x2(1)
    yy(0, 3)
    for k in (1, 2):
        y_rest(0, k)
        to_partner(0, k + 4)
    from_partner(0, 3)
    from_partner(0, 4)
    pointwise(0, 4 * WIDE, 3, 5)
    y_rest(0, 3)
    to_partner(0, 7)
    y_rest(1, 0)
    to_partner(1, 4)
    for k in (5, 6, 7):
        from_partner(0, k)
    pointwise(0, 4 * WIDE, 5, 8)

    def settle(r, _):
        rows = pl.ds(pl.multiple_of(r * WIDE, WIDE), WIDE)
        old = xin[3 + r, 24:72, :].astype(jnp.float32)
        new = (old + scale[0:1, :] * acc[rows, :]).astype(jnp.bfloat16)
        column = mine * OWN - 8 + lax.broadcasted_iota(jnp.int32, (WIDE, C), 0)
        new = jnp.where((column >= 0) & (column < COLS), new, jnp.zeros_like(new))
        state[r, :, :] = new
        for g in range(LANES):
            xf[g, 3 + r, 0:WIDE, :] = new[:, 128 * g : 128 * g + 128].astype(jnp.float32)
        return 0

    lax.fori_loop(0, 4, settle, 0)
    send(state.at[1:4], halo.at[0], h_send.at[0], h_recv.at[0], below)
    send(state.at[0:3], halo.at[1], h_send.at[1], h_recv.at[1], above)
    x1_rest(1)
    for k in (1, 2):
        z(1, k)
        to_partner(1, k)
    for side in range(2):
        arrived(halo.at[side], h_send.at[side], h_recv.at[side])

    @pl.when(row == 0)
    def _():
        halo[0, :, :, :] = jnp.zeros((3, WIDE, C), jnp.bfloat16)

    @pl.when(row == 63)
    def _():
        halo[1, :, :, :] = jnp.zeros((3, WIDE, C), jnp.bfloat16)

    def widen_halo(i, _):
        for side in range(2):
            for g in range(LANES):
                xf[g, 7 * side + i, 0:WIDE, :] = halo[side, i, :, 128 * g : 128 * g + 128].astype(jnp.float32)
        return 0

    lax.fori_loop(0, 3, widen_halo, 0)
    yy(1, 1)
    yy(1, 2)
    convolve(1, OWN, 8)
    pointwise(1, 4 * OWN, 0, 1)
    x2_rest(1)
    z(1, 3)
    to_partner(1, 3)
    for k in (1, 2):
        y_rest(1, k)
        to_partner(1, k + 4)
    from_partner(1, 1)
    from_partner(1, 2)
    pointwise(1, 4 * OWN, 1, 3)
    yy(1, 3)
    from_partner(1, 3)
    from_partner(1, 4)
    pointwise(1, 4 * OWN, 3, 5)
    y_rest(1, 3)
    to_partner(1, 7)
    from_partner(1, 5)
    from_partner(1, 6)
    pointwise(1, 4 * OWN, 5, 7)
    from_partner(1, 7)
    pointwise(1, 4 * OWN, 7, 8)

    def columns_of(h, rows=slice(0, 4)):
        return out.at[rows, pl.ds(pl.multiple_of(place(h) * OWN, OWN), OWN), :]

    def finish(r, _):
        rows = pl.ds(pl.multiple_of(r * OWN, OWN), OWN)
        old = state[r, 8:40, :].astype(jnp.float32)
        new = (old + scale[1:2, :] * acc[rows, :]).astype(jnp.bfloat16)
        out[r, pl.ds(pl.multiple_of(mine * OWN, OWN), OWN), :] = new
        return 0

    lax.fori_loop(0, 4, finish, 0)
    first, second = slice(0, 2), slice(2, 4)

    def get(k, rows, n):
        arrived(columns_of(share(k), rows), g_send.at[n], g_recv.at[n])

    def give(k, rows, n, device):
        pass_on(columns_of(share(k), rows), g_send.at[n], g_recv.at[n], device)

    give(0, slice(0, 4), 0, twin)
    give(0, first, 1, right)
    give(0, second, 3, left)
    give(0, second, 2, right)
    give(0, first, 4, left)
    get(2, first, 1)
    give(2, first, 5, right)
    get(1, second, 3)
    give(1, second, 6, left)
    get(4, slice(0, 4), 0)
    give(4, slice(0, 4), 7, right)
    give(4, slice(0, 4), 8, left)
    get(3, first, 5)
    give(3, first, 9, twin)
    get(3, second, 6)
    give(3, second, 10, twin)
    get(2, second, 2)
    get(1, first, 4)
    get(6, slice(0, 4), 7)
    get(5, slice(0, 4), 8)
    get(7, first, 9)
    get(7, second, 10)
    for copy in sent:
        copy.wait_send()


def tile(features, dw_weight, dw_bias, ln_gain, ln_bias, w_up, b_up, w_down, b_down, layer_scale):
    vmem, anywhere = pl.BlockSpec(memory_space=pltpu.VMEM), pl.BlockSpec(memory_space=pl.ANY)
    dma = pltpu.SemaphoreType.DMA
    pairs = [(2, 4), (2, 2), (2, 4, 2), (2, 4, 2), (2, 7), (7,), (2,), (2,), (11,)]
    return pl.pallas_call(
        kernel,
        out_shape=jax.ShapeDtypeStruct(features.shape, features.dtype),
        in_specs=[anywhere, vmem, vmem, vmem, vmem, anywhere, anywhere, anywhere, vmem, vmem],
        out_specs=vmem,
        scratch_shapes=[
            pltpu.VMEM((2, 8, 2, 512, 256), jnp.bfloat16),
            pltpu.VMEM((8, 2, F), jnp.float32),
            pltpu.VMEM((10, 96, C), jnp.bfloat16),
            pltpu.VMEM((LANES, 10, 64, 128), jnp.float32),
            pltpu.VMEM((4 * WIDE, C), jnp.float32),
            pltpu.VMEM((4 * WIDE, C), jnp.bfloat16),
            pltpu.VMEM((4 * WIDE, C), jnp.float32),
            pltpu.VMEM((4, WIDE, C), jnp.bfloat16),
            pltpu.VMEM((2, 3, WIDE, C), jnp.bfloat16),
            dma((10,)),
            *[dma(shape) for shape in pairs for _ in range(2)],
        ],
        compiler_params=pltpu.CompilerParams(collective_id=0, has_side_effects=True, vmem_limit_bytes=40 << 20),
    )(features, dw_weight, dw_bias, ln_gain, ln_bias, w_up, b_up, w_down, b_down, layer_scale)


def solution(mesh):
    return jax.shard_map(
        tile,
        mesh=mesh,
        in_specs=(
            P("row", None, None),
            P(),
            P(),
            P(),
            P(),
            P(None, None, "hid"),
            P(None, "hid"),
            P(None, "hid", None),
            P(),
            P(),
        ),
        out_specs=P("row", None, None),
        check_vma=False,
    )
```

time: 297 us -> 80.2 us (0.27)
  the two profiles are of different devices: /device:TPU:16 before, /device:TPU:1 now
where the time goes in v1:
time: 80.2 us; the launch traced here: 80 us
  Pallas kernels  74.6 us (93%)
  local copies, waits for them, and re-layouts  5.33 us (7%)
    pallas_call x1, Pallas kernels, tile(): pl.pallas_call(kernel, out_shape=jax.ShapeDtypeStruct(features.shape, fea...  74.6 us
    unnamed x20, local copies, waits for them, and re-layouts  5.33 us

profile of v1, /device:TPU:1, one launch (start us, length us, event | category | flops | bytes accessed | tf_op | source)
XLA Modules:
  0.0 80.0 jit_solution(15767485816199670190)
XLA Ops:
  0.0 0.0 copy-start.7
  0.0 0.0 copy-start.6
  0.0 0.0 copy-start.8
  0.0 0.0 copy-start.5
  0.0 0.0 copy-start.4
  0.0 0.0 copy-start.3
  0.0 1.0 %copy.11.dww = f32[2,7,7,512]{3,2,1,0:T(8,128)S(1)} copy(f32[2,7,7,512]{3,0,2,1:T(2,128)} %param.11) | data formatting | bytes 401408 | tf_op args[1]
  1.1 0.0 copy-done.7
  1.1 0.0 copy-done.6
  1.1 0.0 copy-done.8
  1.1 0.0 copy-done.5
  1.1 0.0 copy-done.4
  1.1 0.0 copy-done.3
  1.1 0.0 copy-start
  1.1 1.2 %copy-done = bf16[4,256,512]{2,1,0:T(8,128)(2,1)S(1)} copy-done((bf16[4,256,512]{2,1,0:T(8,128)(2,1)S(1)}, bf16[4,256,512]{2,1,0:T(8,128)(2,1)}, u32[]{:S(2)}) %copy-start) | copy-done | bytes 1048600
  2.4 0.0 copy-start.1
  2.4 1.0 %copy-done.1 = bf16[2,512,256]{2,1,0:T(8,128)(2,1)S(1)} copy-done((bf16[2,512,256]{2,1,0:T(8,128)(2,1)S(1)}, bf16[2,512,256]{2,1,0:T(8,128)(2,1)}, u32[]{:S(2)}) %copy-start.1) | copy-done | bytes 524312
  3.4 0.0 copy-start.2
  3.4 1.0 %copy-done.2 = bf16[2,256,512]{2,1,0:T(8,128)(2,1)S(1)} copy-done((bf16[2,256,512]{2,1,0:T(8,128)(2,1)S(1)}, bf16[2,256,512]{2,1,0:T(8,128)(2,1)}, u32[]{:S(2)}) %copy-start.2) | copy-done | bytes 524312
  4.4 74.6 %shard_map.100 = bf16[4,256,512]{2,1,0:T(8,128)(2,1)S(1)} custom-call(bf16[4,256,512]{2,1,0:T(8,128)(2,1)S(1)} %copy-done, f32[2,7,7,512]{3,2,1,0:T(8,128)S(1)} %copy.11.dww, f32[2,512]{1,0:T(2,128)S(1)} %copy-done.3, f32[2,512]{1,0:T(2,128)S(1)} %copy-done.4, f32[2,512]{1,0:T(2,128)S(1)} %copy-done.5, bf16[2,512,256]{2,1,0:T(8,128)(2,1)S(1)} %copy-done.1, ...), custom_call_target="tpu_custom_call" | custom-call | tf_op jit(solution)/shard_map/pallas_call | solution.py:361
  79.0 1.0 %copy.13 = bf16[4,256,512]{2,1,0:T(8,128)(2,1)} copy(bf16[4,256,512]{2,1,0:T(8,128)(2,1)S(1)} %shard_map.100) | data formatting | bytes 2097152
Async XLA Ops:
  0.0 1.1 %copy-start.7 = (f32[2,512]{1,0:T(2,128)S(1)}, f32[2,512]{1,0:T(2,128)}, u32[]{:S(2)}) copy-start(f32[2,512]{1,0:T(2,128)} %scale.1) | copy-start | bytes 12292
  0.0 1.1 %copy-start.6 = (f32[2,512]{1,0:T(2,128)S(1)}, f32[2,512]{1,0:T(2,128)}, u32[]{:S(2)}) copy-start(f32[2,512]{1,0:T(2,128)} %b_down.1) | copy-start | bytes 12292
  0.0 1.1 %copy-start.8 = (f32[2,256]{1,0:T(2,128)S(1)}, f32[2,256]{1,0:T(2,128)}, u32[]{:S(2)}) copy-start(f32[2,256]{1,0:T(2,128)} %b_up.1) | copy-start | bytes 6148
  0.0 1.1 %copy-start.5 = (f32[2,512]{1,0:T(2,128)S(1)}, f32[2,512]{1,0:T(2,128)}, u32[]{:S(2)}) copy-start(f32[2,512]{1,0:T(2,128)} %shift.1) | copy-start | bytes 12292
  0.0 1.1 %copy-start.4 = (f32[2,512]{1,0:T(2,128)S(1)}, f32[2,512]{1,0:T(2,128)}, u32[]{:S(2)}) copy-start(f32[2,512]{1,0:T(2,128)} %gain.1) | copy-start | bytes 12292
  0.0 1.1 %copy-start.3 = (f32[2,512]{1,0:T(2,128)S(1)}, f32[2,512]{1,0:T(2,128)}, u32[]{:S(2)}) copy-start(f32[2,512]{1,0:T(2,128)} %dwb.1) | copy-start | bytes 12292
  1.1 1.2 %copy-start = (bf16[4,256,512]{2,1,0:T(8,128)(2,1)S(1)}, bf16[4,256,512]{2,1,0:T(8,128)(2,1)}, u32[]{:S(2)}) copy-start(bf16[4,256,512]{2,1,0:T(8,128)(2,1)} %features.1) | copy-start | bytes 3145732
  2.4 1.0 %copy-start.1 = (bf16[2,512,256]{2,1,0:T(8,128)(2,1)S(1)}, bf16[2,512,256]{2,1,0:T(8,128)(2,1)}, u32[]{:S(2)}) copy-start(bf16[2,512,256]{2,1,0:T(8,128)(2,1)} %w_up.1) | copy-start | bytes 1572868
  3.4 1.0 %copy-start.2 = (bf16[2,256,512]{2,1,0:T(8,128)(2,1)S(1)}, bf16[2,256,512]{2,1,0:T(8,128)(2,1)}, u32[]{:S(2)}) copy-start(bf16[2,256,512]{2,1,0:T(8,128)(2,1)} %w_down.1) | copy-start | bytes 1572868
